TPU v7x, 32 devices: a whole 2x2x4 slice. The times are simulated.
32 devices in a mesh: dp: 8 (over z, x), mp: 4 (over y, core).
Axes of the slice: x: 2, y: 2, z: 4, core: 2. Of those that a mesh axis runs over, the one named last changes fastest.
Arguments:
- inputs: bfloat16 [2, 16384, 768], P(None, ('dp', 'mp')), may hold values from -6 to 6
- lengths: int32 [2, 32], P(None, 'dp'), may hold values from 64 to 512
- membership: int32 [2, 32, 8], replicated, may hold values from 0 to 1, as said below
- w_query: bfloat16 [768, 768], P(None, 'mp'), may hold values from -0.21875 to 0.21875
- b_query: bfloat16 [768], P('mp'), may hold values from -1.75 to 1.75
- w_key: bfloat16 [768, 768], P(None, 'mp'), may hold values from -0.21875 to 0.21875
- w_value: bfloat16 [768, 768], P(None, 'mp'), may hold values from -0.21875 to 0.21875
- b_value: bfloat16 [768], P('mp'), may hold values from -1.75 to 1.75
- w_output: bfloat16 [768, 768], P('mp'), may hold values from -0.875 to 0.875
- b_output: bfloat16 [768], replicated, may hold values from -0.625 to 0.625
- gain_first: bfloat16 [768], replicated, may hold values from 0.5 to 1.5
- bias_first: bfloat16 [768], replicated, may hold values from -0.625 to 0.625
- w_inner: bfloat16 [768, 3072], P(None, 'mp'), may hold values from -0.21875 to 0.21875
- b_inner: bfloat16 [3072], P('mp'), may hold values from -1.75 to 1.75
- w_outer: bfloat16 [3072, 768], P('mp'), may hold values from -0.109375 to 0.109375
- b_outer: bfloat16 [768], replicated, may hold values from -0.625 to 0.625
- gain_second: bfloat16 [768], replicated, may hold values from 0.5 to 1.5
- bias_second: bfloat16 [768], replicated, may hold values from -0.625 to 0.625
Outputs:
- outputs: bfloat16 [2, 16384, 768], P(None, ('dp', 'mp'))
- loss_total: float32 [], replicated
- grad_inputs: float32 [2, 16384, 768], P(None, ('dp', 'mp'))
- grad_w_query: float32 [768, 768], P(None, 'mp')
- grad_b_query: float32 [768], P('mp')
- grad_w_key: float32 [768, 768], P(None, 'mp')
- grad_w_value: float32 [768, 768], P(None, 'mp')
- grad_b_value: float32 [768], P('mp')
- grad_w_output: float32 [768, 768], P('mp')
- grad_b_output: float32 [768], replicated
- grad_gain_first: float32 [768], replicated
- grad_bias_first: float32 [768], replicated
- grad_w_inner: float32 [768, 3072], P(None, 'mp')
- grad_b_inner: float32 [3072], P('mp')
- grad_w_outer: float32 [3072, 768], P('mp')
- grad_b_outer: float32 [768], replicated
- grad_gain_second: float32 [768], replicated
- grad_bias_second: float32 [768], replicated
Inputs may be any that keep to these rules, and one draw needn't show every extreme that they name: `membership`: each row has a single 1. Each of the 8 groups holds 2 to 7 sentences, and some group holds exactly 7 in every draw.
All inputs are finite; a program needn't handle non-finite values.
Results may differ from a plain program's by a relative error of at most 0.015.
Values may be sent and summed in bfloat16 or wider, within the bound.
No kernel may reach another device: no remote copies, remote signals or barrier semaphores. Data moves between devices by JAX's collectives and lax.ppermute only.
A program may use at most 192 MiB of HBM per device.

v0:
```python
import math
import jax
import jax.numpy as jnp
from jax import lax
from jax.sharding import PartitionSpec as P

HEAD_DIM = 64
SEQ_LEN = 512
MICRO = 2
SENT_DEV = 1
eps_norm = 1e-05
eps_unit = 1e-06
cos_scale = 20.0


def layer_norm(row_values, norm_gain, norm_bias):
    centred = row_values - jnp.mean(row_values, axis=-1, keepdims=True)
    spread = jnp.mean(centred * centred, axis=-1, keepdims=True)
    return centred * lax.rsqrt(spread + eps_norm) * norm_gain + norm_bias


def gelu_exact(inner_pre):
    return jax.nn.gelu(inner_pre, approximate=False)


def attend_forward(packed):
    query_rows, key_heads, value_rows, length = packed
    inv_root = 1.0 / math.sqrt(query_rows.shape[-1])
    raw_scores = (
        jnp.einsum("qhd,khd->hqk", query_rows, key_heads, preferred_element_type=jnp.float32)
        * inv_root
    )
    allowed = jnp.arange(raw_scores.shape[-1]) < length
    masked = jnp.where(allowed[None, None, :], raw_scores, -1e30)
    row_top = jnp.max(masked, axis=-1, keepdims=True)
    raised = jnp.exp(masked - row_top)
    sum_all = jnp.sum(raised, axis=-1, keepdims=True)
    prob_low = (raised / sum_all).astype(jnp.bfloat16)
    context = jnp.einsum("hqk,khd->qhd", prob_low, value_rows, preferred_element_type=jnp.float32)
    return (context.astype(jnp.bfloat16), (row_top + jnp.log(sum_all))[:, :, 0])


def attend_backward(packed):
    query_rows, key_heads, value_rows, length, log_total, dcontext_rows = packed
    inv_root = 1.0 / math.sqrt(query_rows.shape[-1])
    raw_scores = (
        jnp.einsum("qhd,khd->hqk", query_rows, key_heads, preferred_element_type=jnp.float32)
        * inv_root
    )
    allowed = jnp.arange(raw_scores.shape[-1]) < length
    prob_rows = jnp.where(allowed[None, None, :], jnp.exp(raw_scores - log_total[:, :, None]), 0.0)
    dprobs = jnp.einsum(
        "qhd,khd->hqk", dcontext_rows, value_rows, preferred_element_type=jnp.float32
    )
    dvalues = jnp.einsum(
        "hqk,qhd->khd",
        prob_rows.astype(jnp.bfloat16),
        dcontext_rows,
        preferred_element_type=jnp.float32,
    )
    weighted = jnp.sum(prob_rows * dprobs, axis=-1, keepdims=True)
    dscores = (prob_rows * (dprobs - weighted)).astype(jnp.bfloat16)
    dqueries = (
        jnp.einsum("hqk,khd->qhd", dscores, key_heads, preferred_element_type=jnp.float32)
        * inv_root
    )
    dkey_heads = (
        jnp.einsum("hqk,qhd->khd", dscores, query_rows, preferred_element_type=jnp.float32)
        * inv_root
    )
    return (
        dqueries.astype(jnp.bfloat16),
        dkey_heads.astype(jnp.bfloat16),
        dvalues.astype(jnp.bfloat16),
    )


def shards(
    inputs,
    lengths,
    membership,
    w_query,
    b_query,
    w_key,
    w_value,
    b_value,
    w_output,
    b_output,
    gain_first,
    bias_first,
    w_inner,
    b_inner,
    w_outer,
    b_outer,
    gain_second,
    bias_second,
):
    groups = lax.axis_size("mp")
    model_rank = lax.axis_index("mp")
    local_width = w_query.shape[1]
    own_rows = inputs.shape[1]
    all_sents = membership.shape[1]
    own_start = (lax.axis_index("dp") * groups + model_rank) * SENT_DEV
    width = inputs.shape[2]
    full_query, full_bquery, full_key, full_value, full_bvalue, full_output = (
        w_query,
        b_query,
        w_key,
        w_value,
        b_value,
        w_output,
    )
    attn_width = full_query.shape[1]
    heads_attn = attn_width // HEAD_DIM
    w_joint = jnp.concatenate([full_query, full_key, full_value], axis=1)
    b_joint = jnp.concatenate([full_bquery, jnp.zeros_like(full_bquery), full_bvalue]).astype(
        jnp.float32
    )
    gain_one = gain_first.astype(jnp.float32)
    bias_one = bias_first.astype(jnp.float32)
    gain_two = gain_second.astype(jnp.float32)
    bias_two = bias_second.astype(jnp.float32)
    shift_output = b_output.astype(jnp.float32)
    shift_outer = b_outer.astype(jnp.float32)
    inner_weight, inner_bias, outer_weight = (w_inner, b_inner, w_outer)
    inner_shift = inner_bias.astype(jnp.float32)
    grad_joint = jnp.zeros(w_joint.shape, jnp.float32)
    grad_bjoint = jnp.zeros(b_joint.shape, jnp.float32)
    grad_wout = jnp.zeros(full_output.shape, jnp.float32)
    grad_inner = jnp.zeros(inner_weight.shape, jnp.float32)
    grad_binner = jnp.zeros(inner_bias.shape, jnp.float32)
    grad_outer = jnp.zeros(outer_weight.shape, jnp.float32)
    grad_boutput = jnp.zeros((width,), jnp.float32)
    grad_bouter = jnp.zeros((width,), jnp.float32)
    grad_gain_one = jnp.zeros((width,), jnp.float32)
    grad_bias_one = jnp.zeros((width,), jnp.float32)
    grad_gain_two = jnp.zeros((width,), jnp.float32)
    grad_bias_two = jnp.zeros((width,), jnp.float32)
    loss_local = jnp.zeros((), jnp.float32)
    outputs_list = []
    grad_list = []
    for micro_index in range(MICRO):
        own_inputs = inputs[micro_index]
        group_lengths = lengths[micro_index]
        own_lengths = lax.dynamic_slice_in_dim(group_lengths, model_rank * SENT_DEV, SENT_DEV)
        gathered = lax.all_gather(own_inputs, "mp", axis=0, tiled=True)
        attn_rows_count = gathered.shape[0]
        attn_sents = attn_rows_count // SEQ_LEN
        joint_rows = (
            jnp.dot(gathered, w_joint, preferred_element_type=jnp.float32) + b_joint
        ).astype(jnp.bfloat16)
        shaped = joint_rows.reshape(attn_sents, SEQ_LEN, 3, heads_attn, HEAD_DIM)
        queries = shaped[:, :, 0]
        key_heads = shaped[:, :, 1]
        values = shaped[:, :, 2]
        context, log_total = lax.map(attend_forward, (queries, key_heads, values, group_lengths))
        context = context.reshape(attn_rows_count, attn_width)
        attn_sum = lax.psum_scatter(
            jnp.dot(context, full_output, preferred_element_type=jnp.float32).astype(jnp.bfloat16),
            "mp",
            scatter_dimension=0,
            tiled=True,
        ).astype(jnp.float32)
        pre_first = attn_sum + shift_output + own_inputs.astype(jnp.float32)
        first_norm = layer_norm(pre_first, gain_one, bias_one)
        first_low = first_norm.astype(jnp.bfloat16)
        ffn_input = lax.all_gather(first_low, "mp", axis=0, tiled=True)
        inner_pre = (
            jnp.dot(ffn_input, inner_weight, preferred_element_type=jnp.float32) + inner_shift
        )
        hidden = gelu_exact(inner_pre).astype(jnp.bfloat16)
        ffn_sum = lax.psum_scatter(
            jnp.dot(hidden, outer_weight, preferred_element_type=jnp.float32).astype(jnp.bfloat16),
            "mp",
            scatter_dimension=0,
            tiled=True,
        ).astype(jnp.float32)
        pre_second = ffn_sum + shift_outer + first_norm
        second_norm = layer_norm(pre_second, gain_two, bias_two)
        outputs_list.append(second_norm.astype(jnp.bfloat16))
        valid_mask = (jnp.arange(SEQ_LEN)[None, :] < own_lengths[:, None]).astype(jnp.float32)
        counts = own_lengths.astype(jnp.float32)[:, None]
        pooled = (
            jnp.sum(second_norm.reshape(SENT_DEV, SEQ_LEN, width) * valid_mask[:, :, None], axis=1)
            / counts
        )
        rscale = lax.rsqrt(jnp.sum(pooled * pooled, axis=1, keepdims=True) + eps_unit)
        unit_rows = pooled * rscale
        every_unit = lax.all_gather(unit_rows, ("dp", "mp"), axis=0, tiled=True)
        groups_all = membership[micro_index].astype(jnp.float32)
        groups_own = lax.dynamic_slice_in_dim(groups_all, own_start, SENT_DEV, 0)
        itself = jnp.arange(all_sents)[None, :] == (own_start + jnp.arange(SENT_DEV))[:, None]
        positive = jnp.where(
            itself, 0.0, jnp.dot(groups_own, groups_all.T, preferred_element_type=jnp.float32)
        )
        logits = cos_scale * jnp.dot(
            unit_rows,
            every_unit.T,
            precision=lax.Precision.HIGHEST,
            preferred_element_type=jnp.float32,
        )
        others = jnp.where(itself, -1e30, logits)
        row_top = jnp.max(others, axis=1, keepdims=True)
        raised = jnp.exp(others - row_top)
        sum_all = jnp.sum(raised, axis=1, keepdims=True)
        sum_pos = jnp.sum(raised * positive, axis=1, keepdims=True)
        loss_local = loss_local + jnp.sum(jnp.log(sum_all) - jnp.log(sum_pos))
        dlogits = raised / sum_all - raised * positive / sum_pos
        dunits = cos_scale * jnp.dot(
            dlogits, every_unit, precision=lax.Precision.HIGHEST, preferred_element_type=jnp.float32
        )
        dkeys_all = cos_scale * jnp.dot(
            dlogits.T,
            unit_rows,
            precision=lax.Precision.HIGHEST,
            preferred_element_type=jnp.float32,
        )
        dunits = dunits + lax.psum_scatter(dkeys_all, ("dp", "mp"), scatter_dimension=0, tiled=True)
        dpooled = rscale * (dunits - unit_rows * jnp.sum(unit_rows * dunits, axis=1, keepdims=True))
        dsecond = ((valid_mask / counts)[:, :, None] * dpooled[:, None, :]).reshape(own_rows, width)
        dpre_second, dgain_two, dbias_two = jax.vjp(layer_norm, pre_second, gain_two, bias_two)[1](
            dsecond
        )
        grad_gain_two = grad_gain_two + dgain_two
        grad_bias_two = grad_bias_two + dbias_two
        grad_bouter = grad_bouter + jnp.sum(dpre_second, axis=0)
        dffn_low = dpre_second.astype(jnp.bfloat16)
        dffn_rows = lax.all_gather(dffn_low, "mp", axis=0, tiled=True)
        grad_outer = grad_outer + jnp.einsum(
            "tf,td->fd", hidden, dffn_rows, preferred_element_type=jnp.float32
        )
        dhidden = jnp.einsum(
            "td,fd->tf", dffn_rows, outer_weight, preferred_element_type=jnp.float32
        )
        dinner = jax.vjp(gelu_exact, inner_pre)[1](dhidden)[0].astype(jnp.bfloat16)
        grad_binner = grad_binner + jnp.sum(dinner, axis=0, dtype=jnp.float32)
        grad_inner = grad_inner + jnp.einsum(
            "td,tf->df", ffn_input, dinner, preferred_element_type=jnp.float32
        )
        dfirst_ffn = lax.psum_scatter(
            jnp.einsum(
                "tf,df->td", dinner, inner_weight, preferred_element_type=jnp.float32
            ).astype(jnp.bfloat16),
            "mp",
            scatter_dimension=0,
            tiled=True,
        ).astype(jnp.float32)
        dfirst = dfirst_ffn + dpre_second
        dpre_first, dgain_one, dbias_one = jax.vjp(layer_norm, pre_first, gain_one, bias_one)[1](
            dfirst
        )
        grad_gain_one = grad_gain_one + dgain_one
        grad_bias_one = grad_bias_one + dbias_one
        grad_boutput = grad_boutput + jnp.sum(dpre_first, axis=0)
        dattn_low = dpre_first.astype(jnp.bfloat16)
        dattn_all = lax.all_gather(dattn_low, "mp", axis=0, tiled=True)
        grad_wout = grad_wout + jnp.einsum(
            "tc,td->cd", context, dattn_all, preferred_element_type=jnp.float32
        )
        dcontext = jnp.einsum(
            "td,cd->tc", dattn_all, full_output, preferred_element_type=jnp.float32
        ).astype(jnp.bfloat16)
        dcontext_heads = dcontext.reshape(attn_sents, SEQ_LEN, heads_attn, HEAD_DIM)
        dqueries, dkey_heads, dvalues = lax.map(
            attend_backward, (queries, key_heads, values, group_lengths, log_total, dcontext_heads)
        )
        djoint = jnp.stack([dqueries, dkey_heads, dvalues], axis=2).reshape(
            attn_rows_count, 3 * attn_width
        )
        grad_bjoint = grad_bjoint + jnp.sum(djoint, axis=0, dtype=jnp.float32)
        grad_joint = grad_joint + jnp.einsum(
            "td,tc->dc", gathered, djoint, preferred_element_type=jnp.float32
        )
        grad_list.append(
            lax.psum_scatter(
                jnp.einsum("tc,dc->td", djoint, w_joint, preferred_element_type=jnp.float32).astype(
                    jnp.bfloat16
                ),
                "mp",
                scatter_dimension=0,
                tiled=True,
            ).astype(jnp.float32)
            + dpre_first
        )
    summed = lax.psum(
        (grad_joint, grad_bjoint, grad_wout, grad_inner, grad_binner, grad_outer), "dp"
    )
    small_sums = lax.psum(
        (
            grad_boutput,
            grad_gain_one,
            grad_bias_one,
            grad_bouter,
            grad_gain_two,
            grad_bias_two,
            loss_local,
        ),
        ("dp", "mp"),
    )
    joint_sum = summed[0]
    bias_sum = summed[1]
    return (
        jnp.stack(outputs_list),
        small_sums[6],
        jnp.stack(grad_list),
        joint_sum[:, :local_width],
        bias_sum[:local_width],
        joint_sum[:, local_width : 2 * local_width],
        joint_sum[:, 2 * local_width :],
        bias_sum[2 * local_width :],
        summed[2],
        small_sums[0],
        small_sums[1],
        small_sums[2],
        summed[3],
        summed[4],
        summed[5],
        small_sums[3],
        small_sums[4],
        small_sums[5],
    )


def solution(mesh):
    placed = (
        P(None, ("dp", "mp"), None),
        P(None, "dp"),
        P(),
        P(None, "mp"),
        P("mp"),
        P(None, "mp"),
        P(None, "mp"),
        P("mp"),
        P("mp", None),
        P(),
        P(),
        P(),
        P(None, "mp"),
        P("mp"),
        P("mp", None),
        P(),
        P(),
        P(),
    )
    return jax.shard_map(
        shards,
        mesh=mesh,
        in_specs=placed,
        out_specs=(
            P(None, ("dp", "mp"), None),
            P(),
            P(None, ("dp", "mp"), None),
            P(None, "mp"),
            P("mp"),
            P(None, "mp"),
            P(None, "mp"),
            P("mp"),
            P("mp", None),
            P(),
            P(),
            P(),
            P(None, "mp"),
            P("mp"),
            P("mp", None),
            P(),
            P(),
            P(),
        ),
        check_vma=False,
    )
```

profile of v0, /device:TPU:0, one launch (start us, length us, event | category | flops | bytes accessed | tf_op | source)
XLA Modules:
  0.0 1240.1 jit_solution(7503602419281284822)
XLA Ops:
  11.6 29.9 %all-gather.27.cloned.1.call-done = bf16[1,2048,768]{2,1,0:T(8,128)(2,1)} async-done(((bf16[1,512,768]{2,1,0:T(8,128)(2,1)}), bf16[1,2048,768]{2,1,0:T(8,128)(2,1)}) %all-gather.27.cloned.1.call-update) | async-done | bytes 3145744 | tf_op jit(solution)/shard_map/all_gather | solution.py:146
  41.5 5.3 fusion.132
  46.8 5.1 reshape.563
  54.9 19.9 %while.52 = (s32[]{:T(128)}, bf16[4,512,3,64]{1,3,2,0:T(8,128)(2,1)}, f32[4,3,512]{2,1,0:T(4,128)}, bf16[4,512,3,64]{1,3,2,0:T(8,128)(2,1)S(1)}, s32[4]{0:T(128)...) while((s32[]{:T(128)}, bf16[4,512,3,64]{1,3,2,0:T(8,128)(2,1)}, ...), condition=%wide.region_3.4_spmd, body=%wide.region_0.3_spmd.sunk | while | flops 210861056 | bytes 10283121 | solution.py:156
  77.4 5.9 fusion.135
  83.3 6.2 reshape.565
  96.7 21.2 %while.53 = (s32[]{:T(128)}, bf16[4,512,3,64]{1,3,2,0:T(8,128)(2,1)S(1)}, f32[4,3,512]{2,1,0:T(4,128)}, bf16[4,512,3,64]{1,3,2,0:T(8,128)(2,1)}, s32[4]{0:T(128)...) while((s32[]{:T(128)}, ...), condition=%wide.region_13.14_spmd, body=%wide.region_10.13_spmd.sunk | while | flops 210861056 | bytes 10283121 | solution.py:156
  123.7 10.4 reduce-scatter.9.cloned.1.call-done
  135.7 39.0 %reduce-scatter.13.cloned.1.call-done = bf16[512,768]{1,0:T(8,128)(2,1)} async-done(((bf16[2048,768]{1,0:T(8,128)(2,1)}), bf16[512,768]{1,0:T(8,128)(2,1)}) %reduce-scatter.13.cloned.1.call-update) | async-done | bytes 786448 | tf_op jit(solution)/shard_map/reduce_scatter | solution.py:158
  182.4 26.8 %all-gather.17.cloned.1.call-done = bf16[2048,768]{1,0:T(8,128)(2,1)} async-done(((bf16[512,768]{1,0:T(8,128)(2,1)}), bf16[2048,768]{1,0:T(8,128)(2,1)}) %all-gather.17.cloned.1.call-update) | async-done | bytes 3145744 | tf_op jit(solution)/shard_map/all_gather | solution.py:167
  209.2 7.2 fusion.212
  216.4 23.4 %all-gather.15.cloned.1.call-done = bf16[2048,768]{1,0:T(8,128)(2,1)} async-done(((bf16[512,768]{1,0:T(8,128)(2,1)}), bf16[2048,768]{1,0:T(8,128)(2,1)}) %all-gather.15.cloned.1.call-update) | async-done | bytes 3145744 | tf_op jit(solution)/shard_map/all_gather | solution.py:167
  239.8 33.0 %multiply_convert_fusion.3 = (bf16[2048,768]{1,0:T(8,128)(2,1)S(1)}, f32[2048,768]{1,0:T(8,128)}, bf16[2048,768]{1,0:T(8,128)(2,1)}, f32[2048,768]{1,0:T(8,128)}, f32[2048,768]{1,0:T(8,128)}) fusion(f32[768]{0:T(1024)} %convert_element_type.270, f32[2048,768]{1,0:T(8,128)} %fusion.212, bf16[2048,768]{1,0:T(8,128)(2,1)} %all-gather.15.cloned.1.call-done, ...), kind=kOutput, calls=%fused_computation.141 | convolution fusion | flops 2623537152 | bytes 35785728 | tf_op jit(solution)/shard_map/dot_general | solution.py:169
  274.5 3.9 convolution_convert_fusion.3
  278.5 6.6 convolution_convert_fusion.2
  300.0 16.6 %reduce-scatter.11.cloned.1.call-done = bf16[512,768]{1,0:T(8,128)(2,1)} async-done(((bf16[2048,768]{1,0:T(8,128)(2,1)}), bf16[512,768]{1,0:T(8,128)(2,1)}) %reduce-scatter.11.cloned.1.call-update) | async-done | bytes 786448 | tf_op jit(solution)/shard_map/reduce_scatter | solution.py:172
  316.6 40.7 %reduce-scatter.15.cloned.1.call-done = bf16[512,768]{1,0:T(8,128)(2,1)} async-done(((bf16[2048,768]{1,0:T(8,128)(2,1)}), bf16[512,768]{1,0:T(8,128)(2,1)}) %reduce-scatter.15.cloned.1.call-update) | async-done | bytes 786448 | tf_op jit(solution)/shard_map/reduce_scatter | solution.py:172
  372.8 40.8 %all-gather.4 = f32[32,1,768]{2,1,0:T(1,128)S(1)} all-gather(f32[1,1,768]{2,1,0:T(1,128)S(1)} %reshape.579), channel_id=4, replica_groups=mesh['dp'=8,'mp'=4] {'dp','mp'}, dimensions={0}, use_global_device_ids=true | all-gather | bytes 101376 | tf_op jit(solution)/shard_map/all_gather | solution.py:189
  413.5 37.1 %all-gather.5 = f32[32,1,768]{2,1,0:T(1,128)S(1)} all-gather(f32[1,1,768]{2,1,0:T(1,128)} %reshape.581), channel_id=5, replica_groups=mesh['dp'=8,'mp'=4] {'dp','mp'}, dimensions={0}, use_global_device_ids=true | all-gather | bytes 101376 | tf_op jit(solution)/shard_map/all_gather | solution.py:189
  468.6 119.6 %all-reduce.9.cloned.1.call-done = (f32[32,768]{1,0:T(8,128)}, f32[32,768]{1,0:T(8,128)}) async-done(((f32[32,768]{1,0:T(8,128)}, f32[32,768]{1,0:T(8,128)}), (f32[32,768]{1,0:T(8,128)}, f32[32,768]{1,0:T(8,128)})) %all-reduce.9.cloned.1.call-update) | async-done | bytes 196624
  594.0 3.9 fusion.145
  606.3 26.3 %all-gather.19.cloned.1.call-done = bf16[2048,768]{1,0:T(8,128)(2,1)} async-done(((bf16[512,768]{1,0:T(8,128)(2,1)}), bf16[2048,768]{1,0:T(8,128)(2,1)}) %all-gather.19.cloned.1.call-update) | async-done | bytes 3145744 | tf_op jit(solution)/shard_map/all_gather | solution.py:228
  632.7 7.6 fusion.213
  640.3 22.6 %all-gather.23.cloned.1.call-done = bf16[2048,768]{1,0:T(8,128)(2,1)} async-done(((bf16[512,768]{1,0:T(8,128)(2,1)}), bf16[2048,768]{1,0:T(8,128)(2,1)}) %all-gather.23.cloned.1.call-update) | async-done | bytes 3145744 | tf_op jit(solution)/shard_map/all_gather | solution.py:228
  662.8 16.7 %convert_reduce_fusion = (f32[768]{0:T(1024)}, bf16[2048,768]{1,0:T(8,128)(2,1)}, f32[768]{0:T(1024)}, bf16[2048,768]{1,0:T(8,128)(2,1)S(1)}) fusion(f32[2048,768]{1,0:T(8,128)} %get-tuple-element.443, f32[2048,768]{1,0:T(8,128)} %fusion.212, f32[768]{0:T(1024)S(1)} %copy-done.87, f32[2048,768]{1,0:T(8,128)} %fusion.213, ...), kind=kOutput, calls=%fused_computation.124 | convolution fusion | flops 2469394944 | bytes 42083328 | tf_op jit(solution)/shard_map/td,fd->tf/dot_general | solution.py:232
  681.1 4.0 convolution_convert_fusion.1
  685.2 6.2 convolution_convert_fusion
  691.6 31.7 %reduce-scatter.17.cloned.1.call-done = bf16[512,768]{1,0:T(8,128)(2,1)} async-done(((bf16[2048,768]{1,0:T(8,128)(2,1)}), bf16[512,768]{1,0:T(8,128)(2,1)}) %reduce-scatter.17.cloned.1.call-update) | async-done | bytes 786448 | tf_op jit(solution)/shard_map/reduce_scatter | solution.py:240
  723.3 40.7 %reduce-scatter.21.cloned.1.call-done = bf16[512,768]{1,0:T(8,128)(2,1)} async-done(((bf16[2048,768]{1,0:T(8,128)(2,1)}), bf16[512,768]{1,0:T(8,128)(2,1)}) %reduce-scatter.21.cloned.1.call-update) | async-done | bytes 786448 | tf_op jit(solution)/shard_map/reduce_scatter | solution.py:240
  764.0 5.1 multiply_reduce_fusion.5
  770.5 4.1 fusion.192
  778.6 27.0 %all-gather.21.cloned.1.call-done = bf16[2048,768]{1,0:T(8,128)(2,1)} async-done(((bf16[512,768]{1,0:T(8,128)(2,1)}), bf16[2048,768]{1,0:T(8,128)(2,1)}) %all-gather.21.cloned.1.call-update) | async-done | bytes 3145744 | tf_op jit(solution)/shard_map/all_gather | solution.py:256
  805.6 3.9 convolution_convert_fusion.9
  812.1 24.0 %all-gather.25.cloned.1.call-done = bf16[2048,768]{1,0:T(8,128)(2,1)} async-done(((bf16[512,768]{1,0:T(8,128)(2,1)}), bf16[2048,768]{1,0:T(8,128)(2,1)}) %all-gather.25.cloned.1.call-update) | async-done | bytes 3145744 | tf_op jit(solution)/shard_map/all_gather | solution.py:256
  836.1 3.9 convolution_convert_fusion.8
  840.1 3.1 reshape.571
  848.2 40.0 %while.55 = (s32[]{:T(128)}, bf16[4,512,3,64]{1,3,2,0:T(8,128)(2,1)}, bf16[4,512,3,64]{1,3,2,0:T(8,128)(2,1)}, bf16[4,512,3,64]{1,3,2,0:T(8,128)(2,1)}, bf16[4,5...) while((s32[]{:T(128)}, ...), condition=%wide.region_51.52_spmd, body=%wide.region_49.51_spmd.sunk | while | flops 510884864 | bytes 25598088 | solution.py:264
  894.3 4.0 convolution_convert_fusion.4
  901.3 36.2 %while.54 = (s32[]{:T(128)}, bf16[4,512,3,64]{1,3,2,0:T(8,128)(2,1)}, bf16[4,512,3,64]{1,3,2,0:T(8,128)(2,1)}, bf16[4,512,3,64]{1,3,2,0:T(8,128)(2,1)}, bf16[4,5...) while((s32[]{:T(128)}, ...), condition=%wide.region_40.41_spmd, body=%wide.region_38.40_spmd.sunk | while | flops 510884864 | bytes 25598088 | solution.py:264
  942.5 4.0 convolution_convert_fusion.5
  947.1 5.7 fusion.216
  956.5 4.2 convolution_add_fusion
  960.7 4.2 convolution_add_fusion.1
  971.2 3.2 add_bitcast_fusion
  984.1 22.7 %all-reduce.4 = (f32[576]{0:T(1024)S(1)}, f32[768]{0:T(1024)}) all-reduce(f32[576]{0:T(1024)S(1)} %add.355, f32[768]{0:T(1024)S(1)} %add.361), channel_id=1, replica_groups=mesh['dp'=8,'mp'=4] {'dp'}, use_global_device_ids=true, to_apply=%region_56.57 | all-reduce | flops 1344 | bytes 10752 | tf_op jit(solution)/shard_map/psum | solution.py:285
  1013.0 41.8 %all-reduce.2 = (f32[]{:T(128)}, f32[768]{0:T(1024)}, f32[768]{0:T(1024)}, f32[768]{0:T(1024)}, f32[768]{0:T(1024)}, /*index=5*/f32[768]{0:T(1024)}, f32[768]{0:T(1024)}) all-reduce(f32[]{:T(128)S(6)} %add.345, f32[768]{0:T(1024)S(1)} %add.357, f32[768]{0:T(1024)S(1)} %add.358, ...), channel_id=1, replica_groups=mesh['dp'=8,'mp'=4] {'dp','mp'}, use_global_device_ids=true, to_apply=%region_30.31 | all-reduce | flops 4609 | bytes 36872 | tf_op jit(solution)/shard_map/psum | solution.py:288
  1054.8 3.8 pad_maximum_fusion
  1058.6 167.9 %all-reduce.11.cloned.1.call-done = (f32[768,576]{0,1:T(8,128)}, f32[192,768]{1,0:T(8,128)}, f32[768,768]{1,0:T(8,128)}, f32[768,768]{1,0:T(8,128)}) async-done(((f32[768,576]{0,1:T(8,128)}, f32[192,768]{1,0:T(8,128)}, f32[768,768]{1,0:T(8,128)}, f32[768,768]{1,0:T(8,128)}), (f32[768,576]{0,1:T(8,128)}, f32[192,768]{1,0:T(8,128)}, f32[768,768]{1,0:T(8,128)}, ...) | async-done | bytes 7077904 | tf_op jit(solution)/shard_map/psum | solution.py:285
  (500 shorter events, 268.0 us)
Async XLA Ops:
  7.2 202.0 %copy-start = (bf16[768,768]{1,0:T(8,128)(2,1)S(1)}, bf16[768,768]{1,0:T(8,128)(2,1)}, u32[]{:S(2)}) copy-start(bf16[768,768]{1,0:T(8,128)(2,1)} %param.38) | copy-start | bytes 3538948
  7.3 34.2 %all-gather.27.cloned.1.call-start = ((), (), s32[]{:S(2)}) async-start(), calls=%async_computation.22 | async-start | bytes 3932160 | tf_op jit(solution)/shard_map/all_gather | solution.py:146
  10.1 67.4 %all-gather.29.cloned.1.call-start = ((), (), s32[]{:S(2)}) async-start(), calls=%async_computation.23 | async-start | bytes 3932160 | tf_op jit(solution)/shard_map/all_gather | solution.py:146
  10.8 123.3 %reduce-scatter.9.cloned.1.call-start = ((), (), s32[]{:S(2)}) async-start(), calls=%async_computation.8 | async-start | bytes 3932160 | tf_op jit(solution)/shard_map/reduce_scatter | solution.py:158
  11.5 30.0 %copy-start.49 = (bf16[768,576]{0,1:T(8,128)(2,1)}, bf16[768,576]{0,1:T(8,128)(2,1)S(1)}, u32[]{:S(2)}) copy-start(bf16[768,576]{0,1:T(8,128)(2,1)S(1)} %constant_dynamic-update-slice_fusion) | copy-start | bytes 2654212
  74.9 8.4 copy-start.12
  74.9 8.4 copy-start.14
  74.9 8.4 copy-start.92
  77.4 15.9 %copy-start.25 = (bf16[24,8,4,512]{3,1,2,0:T(8,128)(2,1)}, bf16[24,8,4,512]{3,1,2,0:T(8,128)(2,1)S(1)}, u32[]{:S(2)}) copy-start(bf16[24,8,4,512]{3,1,2,0:T(8,128)(2,1)S(1)} %copy.108) | copy-start | bytes 2359300
  96.0 78.6 %reduce-scatter.13.cloned.1.call-start = ((), (), s32[]{:S(2)}) async-start(), calls=%async_computation.11 | async-start | bytes 3932160 | tf_op jit(solution)/shard_map/reduce_scatter | solution.py:158
  122.4 11.7 copy-start.1
  122.4 86.8 %all-gather.17.cloned.1.call-start = ((), (), s32[]{:S(2)}) async-start(), calls=%async_computation.12 | async-start | bytes 3932160 | tf_op jit(solution)/shard_map/all_gather | solution.py:167
  134.1 44.3 %copy-start.6 = (bf16[512,768]{1,0:T(8,128)(2,1)S(1)}, bf16[512,768]{1,0:T(8,128)(2,1)}, u32[]{:S(2)}) copy-start(bf16[512,768]{1,0:T(8,128)(2,1)} %reduce-scatter.9.cloned.1.call-done) | copy-start | bytes 2359300
  135.7 221.6 %copy-start.54 = (f32[512]{0:T(512)}, f32[512]{0:T(512)S(1)}, u32[]{:S(2)}) copy-start(f32[512]{0:T(512)S(1)} %broadcast_multiply_fusion.7) | copy-start | bytes 6148
  176.8 180.5 %copy-start.52 = (f32[512]{0:T(512)}, f32[512]{0:T(512)S(1)}, u32[]{:S(2)}) copy-start(f32[512]{0:T(512)S(1)} %broadcast_multiply_fusion.5) | copy-start | bytes 6148
  180.5 59.3 %all-gather.15.cloned.1.call-start = ((), (), s32[]{:S(2)}) async-start(), calls=%async_computation.9 | async-start | bytes 3932160 | tf_op jit(solution)/shard_map/all_gather | solution.py:167
  181.1 135.5 %reduce-scatter.11.cloned.1.call-start = ((), (), s32[]{:S(2)}) async-start(), calls=%async_computation.10 | async-start | bytes 3932160 | tf_op jit(solution)/shard_map/reduce_scatter | solution.py:172
  239.8 34.7 %copy-start.101 = (bf16[768,768]{1,0:T(8,128)(2,1)S(1)}, bf16[768,768]{1,0:T(8,128)(2,1)}, u32[]{:S(2)}) copy-start(bf16[768,768]{1,0:T(8,128)(2,1)} %param.40) | copy-start | bytes 3538948
  278.5 78.8 %reduce-scatter.15.cloned.1.call-start = ((), (), s32[]{:S(2)}) async-start(), calls=%async_computation.13 | async-start | bytes 3932160 | tf_op jit(solution)/shard_map/reduce_scatter | solution.py:172
  285.2 303.1 %all-reduce.9.cloned.1.call-start = ((), (), s32[]{:S(2)}) async-start(), calls=%async_computation.24 | async-start | bytes 393216
  467.3 165.4 %all-gather.19.cloned.1.call-start = ((), (), s32[]{:S(2)}) async-start(), calls=%async_computation.14 | async-start | bytes 3932160 | tf_op jit(solution)/shard_map/all_gather | solution.py:228
  588.2 9.7 copy-start.78
  588.2 9.7 copy-start.76
  588.2 9.7 copy-start.3
  588.2 9.8 copy-start.5
  588.3 9.8 copy-start.57
  588.3 9.8 copy-start.59
  588.3 9.8 copy-start.61
  588.3 9.8 copy-start.67
  588.3 9.8 copy-start.69
  588.3 9.8 copy-start.72
  588.3 9.8 copy-start.73
  603.1 59.8 %all-gather.23.cloned.1.call-start = ((), (), s32[]{:S(2)}) async-start(), calls=%async_computation.18 | async-start | bytes 3932160 | tf_op jit(solution)/shard_map/all_gather | solution.py:228
  603.8 36.5 %copy-start.71 = (f32[512]{0:T(512)}, f32[512]{0:T(512)S(1)}, u32[]{:S(2)}) copy-start(f32[512]{0:T(512)S(1)} %negate_multiply_fusion.3) | copy-start | bytes 6148
  606.3 117.0 %reduce-scatter.17.cloned.1.call-start = ((), (), s32[]{:S(2)}) async-start(), calls=%async_computation.15 | async-start | bytes 3932160 | tf_op jit(solution)/shard_map/reduce_scatter | solution.py:240
  606.3 56.5 %copy-start.87 = (f32[768]{0:T(1024)S(1)}, f32[768]{0:T(1024)}, u32[]{:S(2)}) copy-start(f32[768]{0:T(1024)} %convert_element_type.270) | copy-start | bytes 9220
  685.2 78.8 %reduce-scatter.21.cloned.1.call-start = ((), (), s32[]{:S(2)}) async-start(), calls=%async_computation.19 | async-start | bytes 3932160 | tf_op jit(solution)/shard_map/reduce_scatter | solution.py:240
  691.5 72.5 %copy-start.53 = (f32[512]{0:T(512)S(1)}, f32[512]{0:T(512)}, u32[]{:S(2)}) copy-start(f32[512]{0:T(512)} %copy-done.52) | copy-start | bytes 6148
  691.5 72.5 %copy-start.55 = (f32[512]{0:T(512)S(1)}, f32[512]{0:T(512)}, u32[]{:S(2)}) copy-start(f32[512]{0:T(512)} %copy-done.54) | copy-start | bytes 6148
  691.5 114.0 %all-gather.21.cloned.1.call-start = ((), (), s32[]{:S(2)}) async-start(), calls=%async_computation.16 | async-start | bytes 3932160 | tf_op jit(solution)/shard_map/all_gather | solution.py:256
  775.8 29.8 %copy-start.43 = (bf16[192,768]{1,0:T(8,128)(2,1)S(1)}, bf16[192,768]{1,0:T(8,128)(2,1)}, u32[]{:S(2)}) copy-start(bf16[192,768]{1,0:T(8,128)(2,1)} %param.34) | copy-start | bytes 884740
  776.9 59.3 %all-gather.25.cloned.1.call-start = ((), (), s32[]{:S(2)}) async-start(), calls=%async_computation.20 | async-start | bytes 3932160 | tf_op jit(solution)/shard_map/all_gather | solution.py:256
  778.5 228.3 %reduce-scatter.23.cloned.1.call-start = ((), (), s32[]{:S(2)}) async-start(), calls=%async_computation.21 | async-start | bytes 3932160 | tf_op jit(solution)/shard_map/reduce_scatter | solution.py:275
  809.5 26.6 %copy-start.44 = (bf16[192,768]{1,0:T(8,128)(2,1)S(1)}, bf16[192,768]{1,0:T(8,128)(2,1)}, u32[]{:S(2)}) copy-start(bf16[192,768]{1,0:T(8,128)(2,1)} %param.34) | copy-start | bytes 884740
  898.3 111.6 %reduce-scatter.19.cloned.1.call-start = ((), (), s32[]{:S(2)}) async-start(), calls=%async_computation.17 | async-start | bytes 3932160 | tf_op jit(solution)/shard_map/reduce_scatter | solution.py:275
  946.6 280.0 %all-reduce.11.cloned.1.call-start = ((), (), s32[]{:S(2)}) async-start(), calls=%async_computation.25 | async-start | bytes 14155776 | tf_op jit(solution)/shard_map/psum | solution.py:285
  977.3 32.6 %copy-start.21 = (f32[512,768]{1,0:T(8,128)S(1)}, f32[512,768]{1,0:T(8,128)}, u32[]{:S(2)}) copy-start(f32[512,768]{1,0:T(8,128)} %copy-done.20) | copy-start | bytes 4718596
  979.8 30.1 %copy-start.80 = (f32[512]{0:T(512)S(1)}, f32[512]{0:T(512)}, u32[]{:S(2)}) copy-start(f32[512]{0:T(512)} %copy-done.79) | copy-start | bytes 6148
  (75 other events, 222.3 us)
Sparse Core Ops, SparseCore 0:
  10.2 31.2 all-gather.26
  43.6 28.5 all-gather.28
  96.1 37.9 reduce-scatter.8
  136.7 37.9 reduce-scatter.12
  180.6 28.5 all-gather.16
  211.2 28.5 all-gather.14
  278.6 37.9 reduce-scatter.10
  319.3 37.9 reduce-scatter.14
  467.4 120.8 all-reduce.8
  603.2 29.4 all-gather.18
  634.2 28.5 all-gather.22
  685.3 37.9 reduce-scatter.16
  726.0 37.9 reduce-scatter.20
  777.0 28.5 all-gather.20
  807.5 28.5 all-gather.24
  898.5 37.9 reduce-scatter.22
  946.7 37.9 reduce-scatter.18
  989.6 236.9 all-reduce.10
where the time goes:
time: 1250 us; the launch traced here: 1240 us
  waiting for transfers between devices  648 us (52%)
  matrix products  225 us (18%)
  blocking collectives  142 us (11%)
  other arithmetic  119 us (10%)
  local copies, waits for them, and re-layouts  83.1 us (7%)
  between operations  21.2 us (2%)
    psum x1, waiting for transfers between devices, shards(): lax.psum((grad_joint, grad_bjoint, grad_wout, grad_inner, grad_binner, gr...  168 us
    unnamed x19, waiting for transfers between devices  121 us
    all_gather x2, blocking collectives, shards(): every_unit = lax.all_gather(unit_rows, ('dp', 'mp'), axis=0, tiled=True)  77.9 us
    reduce_scatter x2, waiting for transfers between devices, shards(): lax.psum_scatter(jnp.einsum('tf,df->td', dinner, inner_weight, preferred_...  72.4 us
    reduce_scatter x2, waiting for transfers between devices, shards(): lax.psum_scatter(jnp.dot(hidden, outer_weight, preferred_element_type=jnp...  57.3 us
    all_gather x2, waiting for transfers between devices, shards(): dattn_all = lax.all_gather(dattn_low, 'mp', axis=0, tiled=True)  51 us
    all_gather x2, waiting for transfers between devices, shards(): ffn_input = lax.all_gather(first_low, 'mp', axis=0, tiled=True)  50.2 us
    reduce_scatter x2, waiting for transfers between devices, shards(): lax.psum_scatter(jnp.dot(context, full_output, preferred_element_type=jnp...  49.4 us
  transfers between devices with their start and end apart: 18, of which 15 were waited for; matrix products, arithmetic and copies ran while one was open for 17% of the time, Pallas kernels for 0%

commit v1 on v0

--- a/solution.py
+++ b/solution.py
@@ -143,7 +143,23 @@
         own_inputs = inputs[micro_index]
         group_lengths = lengths[micro_index]
         own_lengths = lax.dynamic_slice_in_dim(group_lengths, model_rank * SENT_DEV, SENT_DEV)
-        gathered = lax.all_gather(own_inputs, "mp", axis=0, tiled=True)
+        parts_n = lax.axis_size("mp")
+        all_rows = []
+        for rr in tuple(range(parts_n)):
+            all_rows.append((rr, (rr + 1) % parts_n))
+        heap = []
+        for rr in tuple(range(parts_n)):
+            heap.append((rr, (rr - 1) % parts_n))
+        current_arr, local_out = ([own_inputs], [own_inputs])
+        for _ in range(parts_n // 2):
+            u_next = lax.ppermute(current_arr[-1], "mp", all_rows)
+            current_arr.append(u_next)
+        for _ in [*range((parts_n - 1) // 2)]:
+            step_out = lax.ppermute(local_out[-1], "mp", heap)
+            local_out.append(step_out)
+        front = jnp.concatenate([*current_arr[::-1], *local_out[1:]], 0)
+        val2 = lax.axis_index("mp")
+        gathered = jnp.roll(front, (val2 - parts_n // 2) * own_inputs.shape[0], 0)
         attn_rows_count = gathered.shape[0]
         attn_sents = attn_rows_count // SEQ_LEN
         joint_rows = (

time: 1250 us -> 1300 us (1.040)
  other arithmetic: 119 us -> 154 us
    concatenate x0 -> x2, other arithmetic: none -> 35.6 us  [shards(): gathered = jnp.roll(front, (val2 - parts_n // 2) * own_inputs.shape[0], 0)]
    ppermute x0 -> x6, waiting for transfers between devices: none -> 32.9 us  [the longest x4 32.9 us: shards(): u_next = lax.ppermute(current_arr[-1], 'mp', all_rows)]
    all_gather x2 -> x0, waiting for transfers between devices: 29.9 us -> none  [shards(): gathered = lax.all_gather(own_inputs, 'mp', axis=0, tiled=True)]
    unnamed x19 -> x17, waiting for transfers between devices: 121 us -> 120 us
  transfers between devices with their start and end apart: 18 -> 22, of which waited for: 15 -> 17; matrix products, arithmetic and copies ran while one was open for 17% -> 18% of each run, Pallas kernels for 0% -> 0%
where the time goes in v1:
time: 1300 us; the launch traced here: 1290 us
  waiting for transfers between devices  653 us (50%)
  matrix products  221 us (17%)
  other arithmetic  154 us (12%)
  blocking collectives  142 us (11%)
  local copies, waits for them, and re-layouts  89.7 us (7%)
  between operations  20.9 us (2%)
    psum x1, waiting for transfers between devices, shards(): lax.psum((grad_joint, grad_bjoint, grad_wout, grad_inner, grad_binner, gr...  168 us
    unnamed x17, waiting for transfers between devices  120 us
    all_gather x2, blocking collectives, shards(): every_unit = lax.all_gather(unit_rows, ('dp', 'mp'), axis=0, tiled=True)  77.9 us
    reduce_scatter x2, waiting for transfers between devices, shards(): lax.psum_scatter(jnp.einsum('tf,df->td', dinner, inner_weight, preferred_...  72.4 us
    reduce_scatter x2, waiting for transfers between devices, shards(): lax.psum_scatter(jnp.dot(hidden, outer_weight, preferred_element_type=jnp...  57.2 us
    reduce_scatter x2, waiting for transfers between devices, shards(): lax.psum_scatter(jnp.dot(context, full_output, preferred_element_type=jnp...  51.7 us
    all_gather x2, waiting for transfers between devices, shards(): dattn_all = lax.all_gather(dattn_low, 'mp', axis=0, tiled=True)  51.1 us
    all_gather x2, waiting for transfers between devices, shards(): ffn_input = lax.all_gather(first_low, 'mp', axis=0, tiled=True)  50.2 us
  transfers between devices with their start and end apart: 22, of which 17 were waited for; matrix products, arithmetic and copies ran while one was open for 18% of the time, Pallas kernels for 0%

profile of v1, /device:TPU:0, one launch (start us, length us, event | category | flops | bytes accessed | tf_op | source)
XLA Modules:
  0.0 1291.2 jit_solution(2133789577934941849)
XLA Ops:
  12.8 14.7 %collective-permute-done = bf16[512,768]{1,0:T(8,128)(2,1)S(1)} collective-permute-done((bf16[512,768]{1,0:T(8,128)(2,1)S(1)}, bf16[512,768]{1,0:T(8,128)(2,1)S(1)}, u32[]{:S(2)}, u32[]{:S(2)}) %collective-permute-start) | collective-permute-done | bytes 786464 | tf_op jit(solution)/shard_map/ppermute | solution.py:155
  33.1 8.8 collective-permute-done.3
  42.0 4.3 collective-permute-start.4
  46.3 9.3 collective-permute-done.1
  55.6 25.7 %fusion.130 = bf16[2048,768]{1,0:T(8,128)(2,1)S(1)} fusion(s32[]{:T(128)S(6)} %select_n.57, bf16[512,768]{1,0:T(8,128)(2,1)} %collective-permute-done.1, bf16[512,768]{1,0:T(8,128)(2,1)S(1)} %collective-permute-done, bf16[512,768]{1,0:T(8,128)(2,1)S(1)} %get-tuple-element.431, bf16[512,768]{1,0:T(8,128)(2,1)S(1)} %collective-permute-done.2), kind=kLoop, calls=%fused_computation.194 | loop fusion | flops 25165824 | bytes 6291460 | tf_op jit(solution)/shard_map/jit(_roll_dynamic)/concatenate | solution.py:162
  86.4 5.3 reshape.563
  94.6 19.9 %while.52 = (s32[]{:T(128)}, bf16[4,512,3,64]{1,3,2,0:T(8,128)(2,1)}, f32[4,3,512]{2,1,0:T(4,128)}, bf16[4,512,3,64]{1,3,2,0:T(8,128)(2,1)S(1)}, s32[4]{0:T(128)...) while((s32[]{:T(128)}, bf16[4,512,3,64]{1,3,2,0:T(8,128)(2,1)}, ...), condition=%wide.region_3.5_spmd, body=%wide.region_0.4_spmd.sunk | while | flops 210861056 | bytes 10283121 | solution.py:172
  117.1 9.9 fusion.123
  132.3 6.4 reshape.565
  145.9 21.1 %while.53 = (s32[]{:T(128)}, bf16[4,512,3,64]{1,3,2,0:T(8,128)(2,1)S(1)}, f32[4,3,512]{2,1,0:T(4,128)}, bf16[4,512,3,64]{1,3,2,0:T(8,128)(2,1)}, s32[4]{0:T(128)...) while((s32[]{:T(128)}, ...), condition=%wide.region_13.15_spmd, body=%wide.region_10.14_spmd.sunk | while | flops 210861056 | bytes 10283121 | solution.py:172
  172.7 12.6 reduce-scatter.9.cloned.1.call-done
  186.9 39.1 %reduce-scatter.13.cloned.1.call-done = bf16[512,768]{1,0:T(8,128)(2,1)} async-done(((bf16[2048,768]{1,0:T(8,128)(2,1)}), bf16[512,768]{1,0:T(8,128)(2,1)}) %reduce-scatter.13.cloned.1.call-update) | async-done | bytes 786448 | tf_op jit(solution)/shard_map/reduce_scatter | solution.py:174
  233.8 26.8 %all-gather.13.cloned.1.call-done = bf16[2048,768]{1,0:T(8,128)(2,1)} async-done(((bf16[512,768]{1,0:T(8,128)(2,1)}), bf16[2048,768]{1,0:T(8,128)(2,1)}) %all-gather.13.cloned.1.call-update) | async-done | bytes 3145744 | tf_op jit(solution)/shard_map/all_gather | solution.py:183
  260.6 7.2 fusion.207
  267.7 23.4 %all-gather.11.cloned.1.call-done = bf16[2048,768]{1,0:T(8,128)(2,1)} async-done(((bf16[512,768]{1,0:T(8,128)(2,1)}), bf16[2048,768]{1,0:T(8,128)(2,1)}) %all-gather.11.cloned.1.call-update) | async-done | bytes 3145744 | tf_op jit(solution)/shard_map/all_gather | solution.py:183
  291.1 33.1 %multiply_convert_fusion.3 = (bf16[2048,768]{1,0:T(8,128)(2,1)S(1)}, f32[2048,768]{1,0:T(8,128)}, bf16[2048,768]{1,0:T(8,128)(2,1)}, f32[2048,768]{1,0:T(8,128)}, f32[2048,768]{1,0:T(8,128)}) fusion(f32[768]{0:T(1024)} %convert_element_type.263, f32[2048,768]{1,0:T(8,128)} %fusion.207, bf16[2048,768]{1,0:T(8,128)(2,1)} %all-gather.11.cloned.1.call-done, ...), kind=kOutput, calls=%fused_computation.157 | convolution fusion | flops 2623537152 | bytes 35785728 | tf_op jit(solution)/shard_map/dot_general | solution.py:185
  326.0 3.9 convolution_convert_fusion.3
  330.0 6.6 convolution_convert_fusion.2
  351.4 16.6 %reduce-scatter.11.cloned.1.call-done = bf16[512,768]{1,0:T(8,128)(2,1)} async-done(((bf16[2048,768]{1,0:T(8,128)(2,1)}), bf16[512,768]{1,0:T(8,128)(2,1)}) %reduce-scatter.11.cloned.1.call-update) | async-done | bytes 786448 | tf_op jit(solution)/shard_map/reduce_scatter | solution.py:188
  368.1 40.5 %reduce-scatter.15.cloned.1.call-done = bf16[512,768]{1,0:T(8,128)(2,1)} async-done(((bf16[2048,768]{1,0:T(8,128)(2,1)}), bf16[512,768]{1,0:T(8,128)(2,1)}) %reduce-scatter.15.cloned.1.call-update) | async-done | bytes 786448 | tf_op jit(solution)/shard_map/reduce_scatter | solution.py:188
  424.1 40.8 %all-gather.2 = f32[32,1,768]{2,1,0:T(1,128)S(1)} all-gather(f32[1,1,768]{2,1,0:T(1,128)S(1)} %reshape.575), channel_id=2, replica_groups=mesh['dp'=8,'mp'=4] {'dp','mp'}, dimensions={0}, use_global_device_ids=true | all-gather | bytes 101376 | tf_op jit(solution)/shard_map/all_gather | solution.py:205
  464.9 37.1 %all-gather.3 = f32[32,1,768]{2,1,0:T(1,128)S(1)} all-gather(f32[1,1,768]{2,1,0:T(1,128)} %reshape.577), channel_id=3, replica_groups=mesh['dp'=8,'mp'=4] {'dp','mp'}, dimensions={0}, use_global_device_ids=true | all-gather | bytes 101376 | tf_op jit(solution)/shard_map/all_gather | solution.py:205
  519.9 119.6 %all-reduce.9.cloned.1.call-done = (f32[32,768]{1,0:T(8,128)}, f32[32,768]{1,0:T(8,128)}) async-done(((f32[32,768]{1,0:T(8,128)}, f32[32,768]{1,0:T(8,128)}), (f32[32,768]{1,0:T(8,128)}, f32[32,768]{1,0:T(8,128)})) %all-reduce.9.cloned.1.call-update) | async-done | bytes 196624
  657.4 26.3 %all-gather.15.cloned.1.call-done = bf16[2048,768]{1,0:T(8,128)(2,1)} async-done(((bf16[512,768]{1,0:T(8,128)(2,1)}), bf16[2048,768]{1,0:T(8,128)(2,1)}) %all-gather.15.cloned.1.call-update) | async-done | bytes 3145744 | tf_op jit(solution)/shard_map/all_gather | solution.py:244
  683.7 7.6 fusion.208
  691.3 22.6 %all-gather.19.cloned.1.call-done = bf16[2048,768]{1,0:T(8,128)(2,1)} async-done(((bf16[512,768]{1,0:T(8,128)(2,1)}), bf16[2048,768]{1,0:T(8,128)(2,1)}) %all-gather.19.cloned.1.call-update) | async-done | bytes 3145744 | tf_op jit(solution)/shard_map/all_gather | solution.py:244
  713.9 16.7 %convert_reduce_fusion = (f32[768]{0:T(1024)}, bf16[2048,768]{1,0:T(8,128)(2,1)}, f32[768]{0:T(1024)}, bf16[2048,768]{1,0:T(8,128)(2,1)S(1)}) fusion(f32[2048,768]{1,0:T(8,128)} %get-tuple-element.444, f32[2048,768]{1,0:T(8,128)} %fusion.207, f32[768]{0:T(1024)S(1)} %copy-done.89, f32[2048,768]{1,0:T(8,128)} %fusion.208, ...), kind=kOutput, calls=%fused_computation.140 | convolution fusion | flops 2469394944 | bytes 42083328 | tf_op jit(solution)/shard_map/td,fd->tf/dot_general | solution.py:248
  732.2 4.0 convolution_convert_fusion.1
  736.3 6.2 convolution_convert_fusion
  742.6 31.7 %reduce-scatter.17.cloned.1.call-done = bf16[512,768]{1,0:T(8,128)(2,1)} async-done(((bf16[2048,768]{1,0:T(8,128)(2,1)}), bf16[512,768]{1,0:T(8,128)(2,1)}) %reduce-scatter.17.cloned.1.call-update) | async-done | bytes 786448 | tf_op jit(solution)/shard_map/reduce_scatter | solution.py:256
  774.3 40.7 %reduce-scatter.21.cloned.1.call-done = bf16[512,768]{1,0:T(8,128)(2,1)} async-done(((bf16[2048,768]{1,0:T(8,128)(2,1)}), bf16[512,768]{1,0:T(8,128)(2,1)}) %reduce-scatter.21.cloned.1.call-update) | async-done | bytes 786448 | tf_op jit(solution)/shard_map/reduce_scatter | solution.py:256
  815.0 5.0 multiply_reduce_fusion.5
  821.5 4.1 fusion.188
  829.6 27.0 %all-gather.17.cloned.1.call-done = bf16[2048,768]{1,0:T(8,128)(2,1)} async-done(((bf16[512,768]{1,0:T(8,128)(2,1)}), bf16[2048,768]{1,0:T(8,128)(2,1)}) %all-gather.17.cloned.1.call-update) | async-done | bytes 3145744 | tf_op jit(solution)/shard_map/all_gather | solution.py:272
  856.5 3.9 convolution_convert_fusion.9
  863.1 24.1 %all-gather.21.cloned.1.call-done = bf16[2048,768]{1,0:T(8,128)(2,1)} async-done(((bf16[512,768]{1,0:T(8,128)(2,1)}), bf16[2048,768]{1,0:T(8,128)(2,1)}) %all-gather.21.cloned.1.call-update) | async-done | bytes 3145744 | tf_op jit(solution)/shard_map/all_gather | solution.py:272
  887.3 3.9 convolution_convert_fusion.8
  899.4 40.0 %while.55 = (s32[]{:T(128)}, bf16[4,512,3,64]{1,3,2,0:T(8,128)(2,1)}, bf16[4,512,3,64]{1,3,2,0:T(8,128)(2,1)}, bf16[4,512,3,64]{1,3,2,0:T(8,128)(2,1)}, bf16[4,5...) while((s32[]{:T(128)}, ...), condition=%wide.region_51.53_spmd, body=%wide.region_49.52_spmd.sunk | while | flops 510884864 | bytes 25598088 | solution.py:280
  945.4 4.0 convolution_convert_fusion.4
  952.4 36.4 %while.54 = (s32[]{:T(128)}, bf16[4,512,3,64]{1,3,2,0:T(8,128)(2,1)}, bf16[4,512,3,64]{1,3,2,0:T(8,128)(2,1)}, bf16[4,512,3,64]{1,3,2,0:T(8,128)(2,1)}, bf16[4,5...) while((s32[]{:T(128)}, ...), condition=%wide.region_40.42_spmd, body=%wide.region_38.41_spmd.sunk | while | flops 510884864 | bytes 25598088 | solution.py:280
  993.9 4.0 convolution_convert_fusion.5
  998.2 5.7 fusion.211
  1007.5 4.2 convolution_add_fusion
  1011.7 4.2 convolution_add_fusion.1
  1035.6 22.8 %all-reduce.4 = (f32[576]{0:T(1024)S(1)}, f32[768]{0:T(1024)}) all-reduce(f32[576]{0:T(1024)S(1)} %add.358, f32[768]{0:T(1024)S(1)} %add.364), channel_id=1, replica_groups=mesh['dp'=8,'mp'=4] {'dp'}, use_global_device_ids=true, to_apply=%region_56.58 | all-reduce | flops 1344 | bytes 10752 | tf_op jit(solution)/shard_map/psum | solution.py:301
  1064.6 41.6 %all-reduce.2 = (f32[]{:T(128)}, f32[768]{0:T(1024)}, f32[768]{0:T(1024)}, f32[768]{0:T(1024)}, f32[768]{0:T(1024)}, /*index=5*/f32[768]{0:T(1024)}, f32[768]{0:T(1024)}) all-reduce(f32[]{:T(128)S(6)} %add.349, f32[768]{0:T(1024)S(1)} %add.360, f32[768]{0:T(1024)S(1)} %add.361, ...), channel_id=1, replica_groups=mesh['dp'=8,'mp'=4] {'dp','mp'}, use_global_device_ids=true, to_apply=%region_30.32 | all-reduce | flops 4609 | bytes 36872 | tf_op jit(solution)/shard_map/psum | solution.py:304
  1106.2 3.8 pad_maximum_fusion
  1110.0 168.0 %all-reduce.11.cloned.1.call-done = (f32[768,576]{0,1:T(8,128)}, f32[192,768]{1,0:T(8,128)}, f32[768,768]{1,0:T(8,128)}, f32[768,768]{1,0:T(8,128)}) async-done(((f32[768,576]{0,1:T(8,128)}, f32[192,768]{1,0:T(8,128)}, f32[768,768]{1,0:T(8,128)}, f32[768,768]{1,0:T(8,128)}), (f32[768,576]{0,1:T(8,128)}, f32[192,768]{1,0:T(8,128)}, f32[768,768]{1,0:T(8,128)}, ...) | async-done | bytes 7077904 | tf_op jit(solution)/shard_map/psum | solution.py:301
  (508 shorter events, 295.4 us)
Async XLA Ops:
  7.2 253.4 %copy-start = (bf16[768,768]{1,0:T(8,128)(2,1)S(1)}, bf16[768,768]{1,0:T(8,128)(2,1)}, u32[]{:S(2)}) copy-start(bf16[768,768]{1,0:T(8,128)(2,1)} %param.40) | copy-start | bytes 3538948
  7.2 22.3 %copy-start.98 = (bf16[192]{0:T(256)(128)(2,1)S(1)}, bf16[192]{0:T(256)(128)(2,1)}, u32[]{:S(2)}) copy-start(bf16[192]{0:T(256)(128)(2,1)} %param.35) | copy-start | bytes 1156
  7.2 22.3 %copy-start.99 = (bf16[192]{0:T(256)(128)(2,1)S(1)}, bf16[192]{0:T(256)(128)(2,1)}, u32[]{:S(2)}) copy-start(bf16[192]{0:T(256)(128)(2,1)} %param.32) | copy-start | bytes 1156
  7.2 25.3 %copy-start.93 = (s32[2,4]{1,0:T(2,128)S(1)}, s32[2,4]{1,0:T(2,128)}, u32[]{:S(2)}) copy-start(s32[2,4]{1,0:T(2,128)} %param.29) | copy-start | bytes 100
  7.2 178.1 %reduce-scatter.9.cloned.1.call-start = ((), (), s32[]{:S(2)}) async-start(), calls=%async_computation.8 | async-start | bytes 3932160 | tf_op jit(solution)/shard_map/reduce_scatter | solution.py:174
  9.7 17.8 %collective-permute-start = (bf16[512,768]{1,0:T(8,128)(2,1)S(1)}, bf16[512,768]{1,0:T(8,128)(2,1)S(1)}, u32[]{:S(2)}, u32[]{:S(2)}) collective-permute-start(bf16[512,768]{1,0:T(8,128)(2,1)S(1)} %get-tuple-element.431), channel_id=1, source_target_pairs={{0,1},{1,2},{2,3},{3,0},{4,5},{5,6},{6,7},{7,4},{8,9},{9,10},{10,1... | collective-permute-start | bytes 2359304 | tf_op jit(solution)/shard_map/ppermute | solution.py:155
  10.2 31.8 %collective-permute-start.3 = (bf16[512,768]{1,0:T(8,128)(2,1)}, bf16[512,768]{1,0:T(8,128)(2,1)}, u32[]{:S(2)}, u32[]{:S(2)}) collective-permute-start(bf16[512,768]{1,0:T(8,128)(2,1)} %get-tuple-element.430), channel_id=1, source_target_pairs={{0,1},{1,2},{2,3},{3,0},{4,5},{5,6},{6,7},{7,4},{8,9},{9,10},{10,1... | collective-permute-start | bytes 2359304 | tf_op jit(solution)/shard_map/ppermute | solution.py:155
  12.8 33.5 %collective-permute-start.2 = (bf16[512,768]{1,0:T(8,128)(2,1)S(1)}, bf16[512,768]{1,0:T(8,128)(2,1)S(1)}, u32[]{:S(2)}, u32[]{:S(2)}) collective-permute-start(bf16[512,768]{1,0:T(8,128)(2,1)S(1)} %get-tuple-element.431), channel_id=1, source_target_pairs={{0,3},{1,0},{2,1},{3,2},{4,7},{5,4},{6,5},{7,6},{8,11},{9,8},{10,9... | collective-permute-start | bytes 2359304 | tf_op jit(solution)/shard_map/ppermute | solution.py:158
  27.5 28.1 %collective-permute-start.1 = (bf16[512,768]{1,0:T(8,128)(2,1)S(1)}, bf16[512,768]{1,0:T(8,128)(2,1)}, u32[]{:S(2)}, u32[]{:S(2)}) collective-permute-start(bf16[512,768]{1,0:T(8,128)(2,1)S(1)} %collective-permute-done), channel_id=1, source_target_pairs={{0,1},{1,2},{2,3},{3,0},{4,5},{5,6},{6,7},{7,4},{8,9},{9,10},{10,1... | collective-permute-start | bytes 2359304 | tf_op jit(solution)/shard_map/ppermute | solution.py:155
  29.5 87.6 %collective-permute-start.5 = (bf16[512,768]{1,0:T(8,128)(2,1)}, bf16[512,768]{1,0:T(8,128)(2,1)}, u32[]{:S(2)}, u32[]{:S(2)}) collective-permute-start(bf16[512,768]{1,0:T(8,128)(2,1)} %get-tuple-element.430), channel_id=1, source_target_pairs={{0,3},{1,0},{2,1},{3,2},{4,7},{5,4},{6,5},{7,6},{8,11},{9,8},{10,9... | collective-permute-start | bytes 2359304 | tf_op jit(solution)/shard_map/ppermute | solution.py:158
  32.6 48.8 %copy-start.50 = (bf16[768,576]{0,1:T(8,128)(2,1)}, bf16[768,576]{0,1:T(8,128)(2,1)S(1)}, u32[]{:S(2)}) copy-start(bf16[768,576]{0,1:T(8,128)(2,1)S(1)} %constant_dynamic-update-slice_fusion) | copy-start | bytes 2654212
  42.0 75.1 %collective-permute-start.4 = (bf16[512,768]{1,0:T(8,128)(2,1)}, bf16[512,768]{1,0:T(8,128)(2,1)}, u32[]{:S(2)}, u32[]{:S(2)}) collective-permute-start(bf16[512,768]{1,0:T(8,128)(2,1)} %collective-permute-done.3), channel_id=1, source_target_pairs={{0,1},{1,2},{2,3},{3,0},{4,5},{5,6},{6,7},{7,4},{8,9},{9,10},{10,1... | collective-permute-start | bytes 2359304 | tf_op jit(solution)/shard_map/ppermute | solution.py:155
  114.5 12.5 copy-start.12
  114.5 12.5 copy-start.14
  114.5 12.5 copy-start.94
  117.1 25.3 %copy-start.25 = (bf16[24,8,4,512]{3,1,2,0:T(8,128)(2,1)}, bf16[24,8,4,512]{3,1,2,0:T(8,128)(2,1)S(1)}, u32[]{:S(2)}) copy-start(bf16[24,8,4,512]{3,1,2,0:T(8,128)(2,1)S(1)} %copy.108) | copy-start | bytes 2359300
  117.1 11.7 copy-start.51
  145.2 80.8 %reduce-scatter.13.cloned.1.call-start = ((), (), s32[]{:S(2)}) async-start(), calls=%async_computation.11 | async-start | bytes 3932160 | tf_op jit(solution)/shard_map/reduce_scatter | solution.py:174
  171.4 13.9 %copy-start.1 = (bf16[2,512,768]{2,1,0:T(8,128)(2,1)S(1)}, bf16[2,512,768]{2,1,0:T(8,128)(2,1)}, u32[]{:S(2)}) copy-start(bf16[2,512,768]{2,1,0:T(8,128)(2,1)} %param.28) | copy-start | bytes 4718596
  171.5 89.1 %all-gather.13.cloned.1.call-start = ((), (), s32[]{:S(2)}) async-start(), calls=%async_computation.12 | async-start | bytes 3932160 | tf_op jit(solution)/shard_map/all_gather | solution.py:183
  185.3 44.5 %copy-start.6 = (bf16[512,768]{1,0:T(8,128)(2,1)S(1)}, bf16[512,768]{1,0:T(8,128)(2,1)}, u32[]{:S(2)}) copy-start(bf16[512,768]{1,0:T(8,128)(2,1)} %reduce-scatter.9.cloned.1.call-done) | copy-start | bytes 2359300
  186.9 221.8 %copy-start.56 = (f32[512]{0:T(512)}, f32[512]{0:T(512)S(1)}, u32[]{:S(2)}) copy-start(f32[512]{0:T(512)S(1)} %broadcast_multiply_fusion.7) | copy-start | bytes 6148
  228.2 180.5 %copy-start.54 = (f32[512]{0:T(512)}, f32[512]{0:T(512)S(1)}, u32[]{:S(2)}) copy-start(f32[512]{0:T(512)S(1)} %broadcast_multiply_fusion.5) | copy-start | bytes 6148
  231.9 59.3 %all-gather.11.cloned.1.call-start = ((), (), s32[]{:S(2)}) async-start(), calls=%async_computation.9 | async-start | bytes 3932160 | tf_op jit(solution)/shard_map/all_gather | solution.py:183
  232.4 135.6 %reduce-scatter.11.cloned.1.call-start = ((), (), s32[]{:S(2)}) async-start(), calls=%async_computation.10 | async-start | bytes 3932160 | tf_op jit(solution)/shard_map/reduce_scatter | solution.py:188
  291.1 34.9 %copy-start.101 = (bf16[768,768]{1,0:T(8,128)(2,1)S(1)}, bf16[768,768]{1,0:T(8,128)(2,1)}, u32[]{:S(2)}) copy-start(bf16[768,768]{1,0:T(8,128)(2,1)} %param.42) | copy-start | bytes 3538948
  330.0 78.6 %reduce-scatter.15.cloned.1.call-start = ((), (), s32[]{:S(2)}) async-start(), calls=%async_computation.13 | async-start | bytes 3932160 | tf_op jit(solution)/shard_map/reduce_scatter | solution.py:188
  336.6 302.9 %all-reduce.9.cloned.1.call-start = ((), (), s32[]{:S(2)}) async-start(), calls=%async_computation.22 | async-start | bytes 393216
  518.6 165.1 %all-gather.15.cloned.1.call-start = ((), (), s32[]{:S(2)}) async-start(), calls=%async_computation.14 | async-start | bytes 3932160 | tf_op jit(solution)/shard_map/all_gather | solution.py:244
  639.6 9.5 copy-start.61
  639.6 9.5 copy-start.63
  639.6 9.5 copy-start.69
  654.1 59.8 %all-gather.19.cloned.1.call-start = ((), (), s32[]{:S(2)}) async-start(), calls=%async_computation.18 | async-start | bytes 3932160 | tf_op jit(solution)/shard_map/all_gather | solution.py:244
  654.8 36.5 %copy-start.73 = (f32[512]{0:T(512)}, f32[512]{0:T(512)S(1)}, u32[]{:S(2)}) copy-start(f32[512]{0:T(512)S(1)} %negate_multiply_fusion.3) | copy-start | bytes 6148
  657.3 117.0 %reduce-scatter.17.cloned.1.call-start = ((), (), s32[]{:S(2)}) async-start(), calls=%async_computation.15 | async-start | bytes 3932160 | tf_op jit(solution)/shard_map/reduce_scatter | solution.py:256
  657.4 56.5 %copy-start.89 = (f32[768]{0:T(1024)S(1)}, f32[768]{0:T(1024)}, u32[]{:S(2)}) copy-start(f32[768]{0:T(1024)} %convert_element_type.263) | copy-start | bytes 9220
  736.3 78.7 %reduce-scatter.21.cloned.1.call-start = ((), (), s32[]{:S(2)}) async-start(), calls=%async_computation.19 | async-start | bytes 3932160 | tf_op jit(solution)/shard_map/reduce_scatter | solution.py:256
  742.5 72.5 %copy-start.55 = (f32[512]{0:T(512)S(1)}, f32[512]{0:T(512)}, u32[]{:S(2)}) copy-start(f32[512]{0:T(512)} %copy-done.54) | copy-start | bytes 6148
  742.5 72.5 %copy-start.57 = (f32[512]{0:T(512)S(1)}, f32[512]{0:T(512)}, u32[]{:S(2)}) copy-start(f32[512]{0:T(512)} %copy-done.56) | copy-start | bytes 6148
  742.6 114.0 %all-gather.17.cloned.1.call-start = ((), (), s32[]{:S(2)}) async-start(), calls=%async_computation.16 | async-start | bytes 3932160 | tf_op jit(solution)/shard_map/all_gather | solution.py:272
  826.8 29.8 %copy-start.47 = (bf16[192,768]{1,0:T(8,128)(2,1)S(1)}, bf16[192,768]{1,0:T(8,128)(2,1)}, u32[]{:S(2)}) copy-start(bf16[192,768]{1,0:T(8,128)(2,1)} %param.36) | copy-start | bytes 884740
  827.8 59.4 %all-gather.21.cloned.1.call-start = ((), (), s32[]{:S(2)}) async-start(), calls=%async_computation.20 | async-start | bytes 3932160 | tf_op jit(solution)/shard_map/all_gather | solution.py:272
  829.5 228.9 %reduce-scatter.23.cloned.1.call-start = ((), (), s32[]{:S(2)}) async-start(), calls=%async_computation.21 | async-start | bytes 3932160 | tf_op jit(solution)/shard_map/reduce_scatter | solution.py:291
  860.5 26.8 %copy-start.48 = (bf16[192,768]{1,0:T(8,128)(2,1)S(1)}, bf16[192,768]{1,0:T(8,128)(2,1)}, u32[]{:S(2)}) copy-start(bf16[192,768]{1,0:T(8,128)(2,1)} %param.36) | copy-start | bytes 884740
  949.5 112.0 %reduce-scatter.19.cloned.1.call-start = ((), (), s32[]{:S(2)}) async-start(), calls=%async_computation.17 | async-start | bytes 3932160 | tf_op jit(solution)/shard_map/reduce_scatter | solution.py:291
  997.9 280.0 %all-reduce.11.cloned.1.call-start = ((), (), s32[]{:S(2)}) async-start(), calls=%async_computation.23 | async-start | bytes 14155776 | tf_op jit(solution)/shard_map/psum | solution.py:301
  1028.8 32.7 %copy-start.21 = (f32[512,768]{1,0:T(8,128)S(1)}, f32[512,768]{1,0:T(8,128)}, u32[]{:S(2)}) copy-start(f32[512,768]{1,0:T(8,128)} %copy-done.20) | copy-start | bytes 4718596
  1031.3 30.2 %copy-start.82 = (f32[512]{0:T(512)S(1)}, f32[512]{0:T(512)}, u32[]{:S(2)}) copy-start(f32[512]{0:T(512)} %copy-done.81) | copy-start | bytes 6148
  (79 other events, 280.1 us)
Sparse Core Ops, SparseCore 0:
  145.3 39.9 reduce-scatter.8
  188.0 37.9 reduce-scatter.12
  232.0 28.5 all-gather.12
  262.6 28.5 all-gather.10
  330.1 37.9 reduce-scatter.10
  370.6 37.9 reduce-scatter.14
  518.7 120.8 all-reduce.8
  654.2 29.4 all-gather.14
  685.3 28.5 all-gather.18
  736.4 37.9 reduce-scatter.16
  777.0 37.9 reduce-scatter.20
  828.0 28.5 all-gather.16
  858.7 28.5 all-gather.20
  949.6 37.9 reduce-scatter.22
  998.0 37.9 reduce-scatter.18
  1040.9 236.9 all-reduce.10
